TPU v7x, 32 devices: a whole 2x2x4 slice. The times are simulated.
32 devices in a mesh: expert: 4 (over z), tensor: 8 (over y, x, core).
Axes of the slice: x: 2, y: 2, z: 4, core: 2. Of those that a mesh axis runs over, the one named last changes fastest.
Arguments:
- tokens: bfloat16 [512, 6144], P('expert', 'tensor'), may hold values from -6 to 6
- out_grad: bfloat16 [512, 6144], P('expert', 'tensor'), may hold values from -6 to 6
- expert_ids: int32 [512, 2], P('expert'), may hold values from 0 to 3, all different within a row; in each aligned block of 128 rows (0 to 127, 128 to 255, ...) at most 80 rows name the same one
- route_logits: float32 [512, 2], P('expert'), may hold values from -6 to 6
- w_gate: bfloat16 [4, 6144, 8192], P('expert', 'tensor'), may hold values from -0.078125 to 0.078125
- w_up: bfloat16 [4, 6144, 8192], P('expert', 'tensor'), may hold values from -0.078125 to 0.078125
- w_down: bfloat16 [4, 6144, 8192], P('expert', 'tensor'), may hold values from -0.0625 to 0.0625
- gate_scale: float32 [4, 8192], P('expert', 'tensor'), may hold values from 0.5 to 2
- up_scale: float32 [4, 8192], P('expert', 'tensor'), may hold values from 0.5 to 2
- down_scale: float32 [4, 8192], P('expert', 'tensor'), may hold values from 0.5 to 2
Outputs:
- mixed: bfloat16 [512, 6144], P('expert', 'tensor')
- token_grad: bfloat16 [512, 6144], P('expert', 'tensor')
- logit_grad: float32 [512, 2], P('expert')
- gate_grad: bfloat16 [4, 6144, 8192], P('expert', None, 'tensor')
- up_grad: bfloat16 [4, 6144, 8192], P('expert', None, 'tensor')
- down_grad: bfloat16 [4, 6144, 8192], P('expert', None, 'tensor')
Inputs may be any that keep to these rules, and one draw needn't show every extreme that they name: `expert_ids`: each token names two different experts; among the 128 tokens of one index of the expert axis, each expert is named by at most 80.
All inputs are finite; a program needn't handle non-finite values.
Results may differ from a plain program's by a relative error of at most 0.025.
Values may be sent and summed in bfloat16 or wider, within the bound.
A program may use at most 256 MiB of HBM per device.

v0:
```python
import jax
import jax.numpy as jnp
from jax import lax
from jax.sharding import PartitionSpec as P


def gate_tables(expert_ids, route_logits, count):
    first = jax.nn.sigmoid(route_logits[:, 0] - route_logits[:, 1])
    probs = jnp.stack([first, 1.0 - first], axis=1)
    labels = jnp.arange(count, dtype=jnp.int32)
    chosen = (expert_ids[:, :, None] == labels[None, None, :]).astype(jnp.float32)
    per_expert = jnp.sum(probs[:, :, None] * chosen, axis=1)
    member = jnp.sum(chosen, axis=1)
    return (probs, chosen, per_expert, member)


def contract_rows(left, right):
    return lax.dot_general(
        left, right, (((0,), (0,)), ((), ())), preferred_element_type=jnp.float32
    )


def body(
    tokens,
    out_grad,
    expert_ids,
    route_logits,
    w_gate,
    w_up,
    w_down,
    gate_scale,
    up_scale,
    down_scale,
):
    groups = lax.axis_size("expert")
    local_tokens, feat_width = tokens.shape
    cap = local_tokens * 5 // 8
    total_rows = groups * cap
    probs, chosen, per_expert, member = gate_tables(expert_ids, route_logits, groups)
    weight_cols = per_expert.T[:, :, None]
    earlier = jnp.tril(jnp.ones((local_tokens, local_tokens), jnp.bfloat16), -1)
    rank = jnp.dot(earlier, member.astype(jnp.bfloat16), preferred_element_type=jnp.float32)
    slots = jnp.arange(cap, dtype=jnp.float32)
    place = jnp.where(
        (member.T[:, None, :] > 0) & (rank.T[:, None, :] == slots[None, :, None]), 1.0, 0.0
    ).astype(jnp.bfloat16)
    weighted = (out_grad.astype(jnp.float32)[None] * weight_cols).astype(jnp.bfloat16)
    send_rows = jnp.einsum("eit,td->eid", place, tokens, preferred_element_type=jnp.float32)
    send_grads = jnp.einsum("eit,etd->eid", place, weighted, preferred_element_type=jnp.float32)
    send = jnp.stack([send_rows, send_grads], axis=1).astype(jnp.bfloat16)
    got = lax.all_to_all(send, "expert", split_axis=0, concat_axis=0, tiled=True)
    rows_loc = got[:, 0].reshape(total_rows, feat_width)
    grads_loc = got[:, 1].reshape(total_rows, feat_width)
    gate_w, up_w, down_w = (w_gate[0], w_up[0], w_down[0])

    def project(left, right):
        part = jnp.dot(left, right, preferred_element_type=jnp.float32).astype(jnp.bfloat16)
        full = lax.psum_scatter(part, "tensor", scatter_dimension=1, tiled=True)
        return full.astype(jnp.float32)

    def gather(value):
        return lax.all_gather(value, "tensor", axis=1, tiled=True)

    def back_project(left, right):
        return lax.dot_general(
            left, right, (((1,), (1,)), ((), ())), preferred_element_type=jnp.float32
        )

    def send_back(value):
        return lax.all_to_all(
            value.astype(jnp.bfloat16).reshape(groups, cap, feat_width),
            "expert",
            split_axis=0,
            concat_axis=0,
            tiled=True,
        )

    gate_pre = project(rows_loc, gate_w) * gate_scale[0]
    up_pre = project(rows_loc, up_w) * up_scale[0]
    back = project(grads_loc, down_w) * down_scale[0]
    rows_in = gather(rows_loc)
    grads_in = gather(grads_loc)
    sigma = jax.nn.sigmoid(gate_pre)
    active = gate_pre * sigma
    hidden = (active * up_pre * down_scale[0]).astype(jnp.bfloat16)
    d_gate = (back * up_pre * sigma * (1.0 + gate_pre * (1.0 - sigma)) * gate_scale[0]).astype(
        jnp.bfloat16
    )
    d_up = (back * active * up_scale[0]).astype(jnp.bfloat16)
    out_back = send_back(back_project(gather(hidden), down_w))
    grad_back = send_back(back_project(gather(d_gate), gate_w) + back_project(gather(d_up), up_w))
    down_grad = contract_rows(grads_in, hidden).astype(jnp.bfloat16)
    gate_grad = contract_rows(rows_in, d_gate).astype(jnp.bfloat16)
    up_grad = contract_rows(rows_in, d_up).astype(jnp.bfloat16)
    out_float = jnp.einsum("eit,eid->etd", place, out_back, preferred_element_type=jnp.float32)
    token_grad = lax.dot_general(
        place.reshape(total_rows, local_tokens),
        grad_back.reshape(total_rows, feat_width),
        (((0,), (0,)), ((), ())),
        preferred_element_type=jnp.float32,
    ).astype(jnp.bfloat16)
    mixed = jnp.sum(weight_cols * out_float, axis=0).astype(jnp.bfloat16)
    local_score = jnp.einsum("td,etd->te", out_grad.astype(jnp.float32), out_float)
    score = lax.psum(local_score, "tensor")
    pick = jnp.sum(chosen * score[:, None, :], axis=2)
    mean_pick = jnp.sum(probs * pick, axis=1, keepdims=True)
    logit_grad = probs * (pick - mean_pick)
    return (mixed, token_grad, logit_grad, gate_grad[None], up_grad[None], down_grad[None])


def solution(mesh):
    in_specs = (
        P("expert", "tensor"),
        P("expert", "tensor"),
        P("expert", None),
        P("expert", None),
        P("expert", "tensor", None),
        P("expert", "tensor", None),
        P("expert", "tensor", None),
        P("expert", "tensor"),
        P("expert", "tensor"),
        P("expert", "tensor"),
    )
    out_specs = (
        P("expert", "tensor"),
        P("expert", "tensor"),
        P("expert", None),
        P("expert", None, "tensor"),
        P("expert", None, "tensor"),
        P("expert", None, "tensor"),
    )
    return jax.shard_map(body, mesh=mesh, in_specs=in_specs, out_specs=out_specs, check_vma=False)
```

profile of v0, /device:TPU:0, one launch (start us, length us, event | category | flops | bytes accessed | tf_op | source)
XLA Modules:
  0.0 471.8 jit_solution(13692234341856689508)
XLA Ops:
  10.7 30.5 %all_to_all.15 = bf16[4,2,80,768]{3,2,1,0:T(8,128)(2,1)S(1)} all-to-all(bf16[4,2,80,768]{3,2,1,0:T(8,128)(2,1)S(1)} %copy.21), channel_id=1, replica_groups=mesh['expert'=4,'tensor'=8] {'expert'}, dimensions={0} | all-to-all | bytes 1966080 | tf_op jit(solution)/shard_map/all_to_all | solution.py:51
  41.3 10.9 %fusion.18 = bf16[320,8192]{1,0:T(8,128)(2,1)} fusion(bf16[320,768]{1,0:T(8,128)(2,1)S(1)} %bitcast.70, bf16[1,768,8192]{2,1,0:T(8,128)(2,1)} %param.16), kind=kOutput, calls=%fused_computation.17 | convolution fusion | flops 4029153280 | bytes 18317312 | tf_op jit(solution)/shard_map/dot_general | solution.py:57
  52.3 10.6 %fusion.15 = bf16[320,8192]{1,0:T(8,128)(2,1)} fusion(bf16[320,768]{1,0:T(8,128)(2,1)S(1)} %bitcast.72, bf16[1,768,8192]{2,1,0:T(8,128)(2,1)} %param.15), kind=kOutput, calls=%fused_computation.16 | convolution fusion | flops 4029153280 | bytes 18317312 | tf_op jit(solution)/shard_map/dot_general | solution.py:57
  63.0 11.2 %fusion.12 = bf16[320,8192]{1,0:T(8,128)(2,1)} fusion(bf16[320,768]{1,0:T(8,128)(2,1)S(1)} %bitcast.73, bf16[1,768,8192]{2,1,0:T(8,128)(2,1)} %param.14), kind=kOutput, calls=%fused_computation.15 | convolution fusion | flops 4029153280 | bytes 18317312 | tf_op jit(solution)/shard_map/dot_general | solution.py:57
  75.5 32.4 %reduce-scatter.8.cloned.1.call-done = bf16[320,1024]{1,0:T(8,128)(2,1)} async-done(((bf16[320,8192]{1,0:T(8,128)(2,1)}), bf16[320,1024]{1,0:T(8,128)(2,1)}) %reduce-scatter.8.cloned.1.call-update) | async-done | bytes 655376 | tf_op jit(solution)/shard_map/reduce_scatter | solution.py:58
  107.9 60.4 %reduce-scatter.6.cloned.1.call-done = bf16[320,1024]{1,0:T(8,128)(2,1)} async-done(((bf16[320,8192]{1,0:T(8,128)(2,1)}), bf16[320,1024]{1,0:T(8,128)(2,1)}) %reduce-scatter.6.cloned.1.call-update) | async-done | bytes 655376 | tf_op jit(solution)/shard_map/reduce_scatter | solution.py:58
  168.3 60.4 %reduce-scatter.4.cloned.1.call-done = bf16[320,1024]{1,0:T(8,128)(2,1)} async-done(((bf16[320,8192]{1,0:T(8,128)(2,1)}), bf16[320,1024]{1,0:T(8,128)(2,1)}) %reduce-scatter.4.cloned.1.call-update) | async-done | bytes 655376 | tf_op jit(solution)/shard_map/reduce_scatter | solution.py:58
  228.7 3.6 multiply_convert_fusion.2
  233.9 32.0 %all-gather.12.cloned.1.call-done = bf16[320,6144]{1,0:T(8,128)(2,1)} async-done(((bf16[320,768]{1,0:T(8,128)(2,1)}), bf16[320,6144]{1,0:T(8,128)(2,1)}) %all-gather.12.cloned.1.call-update) | async-done | bytes 3932176 | tf_op jit(solution)/shard_map/all_gather | solution.py:62
  265.9 12.1 %convert_bitcast_fusion.2 = bf16[1,6144,1024]{2,1,0:T(8,128)(2,1)} fusion(bf16[320,6144]{1,0:T(8,128)(2,1)} %all-gather.12.cloned.1.call-done, bf16[320,1024]{1,0:T(8,128)(2,1)} %get-tuple-element.10), kind=kOutput, calls=%fused_computation.14 | convolution fusion | flops 4032823296 | bytes 17170432 | tf_op jit(solution)/shard_map/dot_general | solution.py:18
  278.0 9.7 %convert_bitcast_fusion.1 = bf16[1,6144,1024]{2,1,0:T(8,128)(2,1)} fusion(bf16[320,6144]{1,0:T(8,128)(2,1)S(1)} %copy-done.11, bf16[320,1024]{1,0:T(8,128)(2,1)S(1)} %copy-done.2), kind=kOutput, calls=%fused_computation.13 | convolution fusion | flops 4032823296 | bytes 17170432 | tf_op jit(solution)/shard_map/dot_general | solution.py:18
  287.7 15.4 %all-gather.14.cloned.1.call-done = bf16[320,6144]{1,0:T(8,128)(2,1)} async-done(((bf16[320,768]{1,0:T(8,128)(2,1)}), bf16[320,6144]{1,0:T(8,128)(2,1)}) %all-gather.14.cloned.1.call-update) | async-done | bytes 3932176 | tf_op jit(solution)/shard_map/all_gather | solution.py:62
  303.1 11.8 %convert_bitcast_fusion = bf16[1,6144,1024]{2,1,0:T(8,128)(2,1)} fusion(bf16[320,6144]{1,0:T(8,128)(2,1)} %all-gather.14.cloned.1.call-done, bf16[320,1024]{1,0:T(8,128)(2,1)S(1)} %copy-done.3), kind=kOutput, calls=%fused_computation.12 | convolution fusion | flops 4032823296 | bytes 17170432 | tf_op jit(solution)/shard_map/dot_general | solution.py:18
  314.9 31.0 %all-gather.6.cloned.1.call-done = bf16[320,8192]{1,0:T(8,128)(2,1)} async-done(((bf16[320,1024]{1,0:T(8,128)(2,1)}), bf16[320,8192]{1,0:T(8,128)(2,1)}) %all-gather.6.cloned.1.call-update) | async-done | bytes 5242896 | tf_op jit(solution)/shard_map/all_gather | solution.py:62
  345.9 11.2 %fusion.30 = bf16[320,768]{1,0:T(8,128)(2,1)} fusion(bf16[320,8192]{1,0:T(8,128)(2,1)} %all-gather.6.cloned.1.call-done, bf16[1,768,8192]{2,1,0:T(8,128)(2,1)} %param.16), kind=kOutput, calls=%fused_computation.32 | convolution fusion | flops 4026777600 | bytes 18317312 | tf_op jit(solution)/shard_map/dot_general | solution.py:65
  357.1 4.6 all-to-all-start.1
  361.7 27.1 %all-gather.10.cloned.1.call-done = bf16[320,8192]{1,0:T(8,128)(2,1)} async-done(((bf16[320,1024]{1,0:T(8,128)(2,1)}), bf16[320,8192]{1,0:T(8,128)(2,1)}) %all-gather.10.cloned.1.call-update) | async-done | bytes 5242896 | tf_op jit(solution)/shard_map/all_gather | solution.py:62
  388.8 9.1 %fusion.4 = f32[320,768]{1,0:T(8,128)S(1)} fusion(bf16[320,8192]{1,0:T(8,128)(2,1)} %all-gather.10.cloned.1.call-done, bf16[1,768,8192]{2,1,0:T(8,128)(2,1)} %param.15), kind=kOutput, calls=%fused_computation.4 | convolution fusion | flops 4026531840 | bytes 18808832 | tf_op jit(solution)/shard_map/dot_general | solution.py:65
  397.9 33.8 %all-gather.8.cloned.1.call-done = bf16[320,8192]{1,0:T(8,128)(2,1)} async-done(((bf16[320,1024]{1,0:T(8,128)(2,1)}), bf16[320,8192]{1,0:T(8,128)(2,1)}) %all-gather.8.cloned.1.call-update) | async-done | bytes 5242896 | tf_op jit(solution)/shard_map/all_gather | solution.py:62
  431.7 11.3 %fusion.27 = bf16[320,768]{1,0:T(8,128)(2,1)} fusion(f32[320,768]{1,0:T(8,128)S(1)} %fusion.4, bf16[320,8192]{1,0:T(8,128)(2,1)} %all-gather.8.cloned.1.call-done, bf16[1,768,8192]{2,1,0:T(8,128)(2,1)} %param.14), kind=kOutput, calls=%fused_computation.31 | convolution fusion | flops 4027023360 | bytes 19300352 | tf_op jit(solution)/shard_map/dot_general | solution.py:65
  443.0 4.7 %all-to-all-start.2 = ((bf16[4,80,768]{2,1,0:T(8,128)(2,1)}), bf16[4,80,768]{2,1,0:T(8,128)(2,1)S(1)}, u32[]{:S(2)}, u32[]{:S(2)}) async-start(bf16[4,80,768]{2,1,0:T(8,128)(2,1)} %bitcast.14), calls=%async_computation.5 | async-start | bytes 983040 | tf_op jit(solution)/shard_map/all_to_all | solution.py:70
  447.7 1.1 multiply_reduce_fusion
  448.8 1.1 fusion.21
  449.9 13.4 %psum.7 = f32[128,4]{0,1:T(4,128)S(1)} all-reduce(f32[128,4]{0,1:T(4,128)S(1)} %bitcast.78), channel_id=1, replica_groups=mesh['expert'=4,'tensor'=8] {'tensor'}, use_global_device_ids=true, to_apply=%region_6.7 | all-reduce | flops 512 | bytes 4096 | tf_op jit(solution)/shard_map/psum | solution.py:104
  (59 shorter events, 8.1 us)
Async XLA Ops:
  7.2 2.7 copy-start
  7.2 100.7 %reduce-scatter.8.cloned.1.call-start = ((), (), s32[]{:S(2)}) async-start(), calls=%async_computation.9 | async-start | bytes 5898240 | tf_op jit(solution)/shard_map/reduce_scatter | solution.py:58
  41.3 11.0 %copy-start.4 = (bf16[4,1,80,768]{3,2,1,0:T(8,128)(2,1)}, bf16[4,1,80,768]{3,2,1,0:T(8,128)(2,1)S(1)}, u32[]{:S(2)}) copy-start(bf16[4,1,80,768]{3,2,1,0:T(8,128)(2,1)S(1)} %get-tuple-element.13) | copy-start | bytes 1474564
  41.3 21.7 %copy-start.5 = (bf16[4,1,80,768]{3,2,1,0:T(8,128)(2,1)}, bf16[4,1,80,768]{3,2,1,0:T(8,128)(2,1)S(1)}, u32[]{:S(2)}) copy-start(bf16[4,1,80,768]{3,2,1,0:T(8,128)(2,1)S(1)} %get-tuple-element.14) | copy-start | bytes 1474564
  52.3 116.0 %reduce-scatter.6.cloned.1.call-start = ((), (), s32[]{:S(2)}) async-start(), calls=%async_computation.7 | async-start | bytes 5898240 | tf_op jit(solution)/shard_map/reduce_scatter | solution.py:58
  63.0 165.7 %reduce-scatter.4.cloned.1.call-start = ((), (), s32[]{:S(2)}) async-start(), calls=%async_computation.6 | async-start | bytes 5898240 | tf_op jit(solution)/shard_map/reduce_scatter | solution.py:58
  74.2 154.5 %copy-start.7 = (f32[1,1024]{1,0:T(1,128)S(1)}, f32[1,1024]{1,0:T(1,128)}, u32[]{:S(2)}) copy-start(f32[1,1024]{1,0:T(1,128)} %param.19) | copy-start | bytes 12292
  74.2 154.5 %copy-start.8 = (f32[1,1024]{1,0:T(1,128)S(1)}, f32[1,1024]{1,0:T(1,128)}, u32[]{:S(2)}) copy-start(f32[1,1024]{1,0:T(1,128)} %param.18) | copy-start | bytes 12292
  74.3 154.5 %copy-start.9 = (f32[1,1024]{1,0:T(1,128)S(1)}, f32[1,1024]{1,0:T(1,128)}, u32[]{:S(2)}) copy-start(f32[1,1024]{1,0:T(1,128)} %param.17) | copy-start | bytes 12292
  74.3 191.6 %all-gather.12.cloned.1.call-start = ((), (), s32[]{:S(2)}) async-start(), calls=%async_computation.12 | async-start | bytes 4423680 | tf_op jit(solution)/shard_map/all_gather | solution.py:62
  74.9 228.2 %all-gather.14.cloned.1.call-start = ((), (), s32[]{:S(2)}) async-start(), calls=%async_computation.13 | async-start | bytes 4423680 | tf_op jit(solution)/shard_map/all_gather | solution.py:62
  75.4 270.4 %all-gather.6.cloned.1.call-start = ((), (), s32[]{:S(2)}) async-start(), calls=%async_computation.8 | async-start | bytes 5898240 | tf_op jit(solution)/shard_map/all_gather | solution.py:62
  232.4 156.4 %all-gather.10.cloned.1.call-start = ((), (), s32[]{:S(2)}) async-start(), calls=%async_computation.11 | async-start | bytes 5898240 | tf_op jit(solution)/shard_map/all_gather | solution.py:62
  233.1 198.6 %all-gather.8.cloned.1.call-start = ((), (), s32[]{:S(2)}) async-start(), calls=%async_computation.10 | async-start | bytes 5898240 | tf_op jit(solution)/shard_map/all_gather | solution.py:62
  233.9 44.1 %copy-start.2 = (bf16[320,1024]{1,0:T(8,128)(2,1)S(1)}, bf16[320,1024]{1,0:T(8,128)(2,1)}, u32[]{:S(2)}) copy-start(bf16[320,1024]{1,0:T(8,128)(2,1)} %get-tuple-element.12) | copy-start | bytes 1966084
  265.9 12.1 %copy-start.11 = (bf16[320,6144]{1,0:T(8,128)(2,1)S(1)}, bf16[320,6144]{1,0:T(8,128)(2,1)}, u32[]{:S(2)}) copy-start(bf16[320,6144]{1,0:T(8,128)(2,1)} %all-gather.12.cloned.1.call-done) | copy-start | bytes 11796484
  278.0 25.1 %copy-start.3 = (bf16[320,1024]{1,0:T(8,128)(2,1)S(1)}, bf16[320,1024]{1,0:T(8,128)(2,1)}, u32[]{:S(2)}) copy-start(bf16[320,1024]{1,0:T(8,128)(2,1)} %get-tuple-element.11) | copy-start | bytes 1966084
  357.1 85.9 %all-to-all-start.1 = ((bf16[4,80,768]{2,1,0:T(8,128)(2,1)}), bf16[4,80,768]{2,1,0:T(8,128)(2,1)S(1)}, u32[]{:S(2)}, u32[]{:S(2)}) async-start(bf16[4,80,768]{2,1,0:T(8,128)(2,1)} %bitcast.12), calls=%async_computation.3 | async-start | bytes 983040 | tf_op jit(solution)/shard_map/all_to_all | solution.py:70
  397.9 50.9 %copy-start.6 = (bf16[128,768]{1,0:T(8,128)(2,1)S(1)}, bf16[128,768]{1,0:T(8,128)(2,1)}, u32[]{:S(2)}) copy-start(bf16[128,768]{1,0:T(8,128)(2,1)} %param.11) | copy-start | bytes 589828
  431.7 33.3 %copy-start.1 = (bf16[128,768]{1,0:T(8,128)(2,1)S(1)}, bf16[128,768]{1,0:T(8,128)(2,1)}, u32[]{:S(2)}) copy-start(bf16[128,768]{1,0:T(8,128)(2,1)} %param.10) | copy-start | bytes 589828
  443.0 20.4 %copy-start.10 = (s32[128,2]{0,1:T(2,128)S(1)}, s32[128,2]{0,1:T(2,128)}, u32[]{:S(2)}) copy-start(s32[128,2]{0,1:T(2,128)} %param.12) | copy-start | bytes 3076
  443.0 21.0 %all-to-all-start.2 = ((bf16[4,80,768]{2,1,0:T(8,128)(2,1)}), bf16[4,80,768]{2,1,0:T(8,128)(2,1)S(1)}, u32[]{:S(2)}, u32[]{:S(2)}) async-start(bf16[4,80,768]{2,1,0:T(8,128)(2,1)} %bitcast.14), calls=%async_computation.5 | async-start | bytes 983040 | tf_op jit(solution)/shard_map/all_to_all | solution.py:70
Sparse Core Ops, SparseCore 0:
  52.4 55.4 reduce-scatter.7
  111.9 56.3 reduce-scatter.5
  172.3 56.3 reduce-scatter.3
  230.5 35.4 all-gather.11
  267.7 35.3 all-gather.13
  304.9 40.9 all-gather.5
  347.8 40.9 all-gather.9
  390.7 40.9 all-gather.7
where the time goes:
time: 472 us
  waiting for transfers between devices  295 us (62%)
  matrix products  102 us (22%)
  blocking collectives  43.9 us (9%)
  between operations  14.3 us (3%)
  starting transfers between devices  9.82 us (2%)
  other arithmetic  6.8 us (1%)
    reduce_scatter x3, waiting for transfers between devices, project(): full = lax.psum_scatter(part, 'tensor', scatter_dimension=1, tiled=True)  153 us
    all_gather x5, waiting for transfers between devices, gather(): return lax.all_gather(value, 'tensor', axis=1, tiled=True)  139 us
    dot_general x3, matrix products, contract_rows(): lax.dot_general(left, right, (((0,), (0,)), ((), ())), preferred_element_...  33.6 us
    dot_general x3, matrix products, project(): jnp.dot(left, right, preferred_element_type=jnp.float32)  32.8 us
    dot_general x3, matrix products, back_project(): lax.dot_general(left, right, (((1,), (1,)), ((), ())), preferred_element_...  31.6 us
    all_to_all x1, blocking collectives, body(): lax.all_to_all(send, 'expert', split_axis=0, concat_axis=0, tiled=True)  30.5 us
    psum x1, blocking collectives, body(): score = lax.psum(local_score, 'tensor')  13.4 us
  transfers between devices with their start and end apart: 10, of which 8 were waited for; matrix products, arithmetic and copies ran while one was open for 20% of the time, Pallas kernels for 0%

commit v1 on v0

--- a/solution.py
+++ b/solution.py
@@ -59,7 +59,24 @@
         return full.astype(jnp.float32)
 
     def gather(value):
-        return lax.all_gather(value, "tensor", axis=1, tiled=True)
+
+        def render_the_limits(target, where_dim):
+            net_axis = "tensor"
+            s_next = lax.axis_size(net_axis)
+            mid_arr = lax.axis_index(net_axis)
+            current_arr, prior, finding = (s_next, mid_arr, target.shape[where_dim])
+            w2, base_arr = (target, 1)
+            while base_arr < current_arr:
+                value_now = lax.ppermute(
+                    w2,
+                    axis_name=net_axis,
+                    perm=[(pp, (pp - base_arr) % current_arr) for pp in range(current_arr)],
+                )
+                w2 = jnp.concatenate([w2, value_now], axis=where_dim)
+                base_arr = 2 * base_arr
+            return jnp.roll(w2, prior * finding, axis=where_dim)
+
+        return render_the_limits(value, 1)
 
     def back_project(left, right):
         return lax.dot_general(

time: 472 us -> 643 us (1.36); the launches traced: 472 us -> 635 us
  blocking collectives: 43.9 us -> 104 us
  matrix products: 102 us -> 131 us
  waiting for transfers between devices: 295 us -> 323 us
  other arithmetic: 6.8 us -> 33.2 us
  starting transfers between devices: 9.82 us -> 26.3 us
    ppermute x0 -> x15, waiting for transfers between devices: none -> 173 us  [render_the_limits(): lax.ppermute(w2, axis_name=net_axis, perm=[(pp, (pp - base_arr) % current...]
    all_gather x5 -> x0, waiting for transfers between devices: 139 us -> none  [gather(): return lax.all_gather(value, 'tensor', axis=1, tiled=True)]
    psum x1, blocking collectives: 13.4 us -> 73.9 us  [body(): score = lax.psum(local_score, 'tensor')]
    concatenate x0 -> x11, other arithmetic: none -> 27.5 us  [the longest x10 14.6 us: render_the_limits(): w2 = jnp.concatenate([w2, value_now], axis=where_dim)]
    dot_general x3, matrix products: 31.6 us -> 56.5 us  [back_project(): lax.dot_general(left, right, (((1,), (1,)), ((), ())), preferred_element_...]
    ppermute x0 -> x15, starting transfers between devices: none -> 16.8 us  [render_the_limits(): lax.ppermute(w2, axis_name=net_axis, perm=[(pp, (pp - base_arr) % current...]
  transfers between devices with their start and end apart: 10 -> 20, of which waited for: 8 -> 10; matrix products, arithmetic and copies ran while one was open for 20% -> 24% of each run, Pallas kernels for 0% -> 0%
where the time goes in v1:
time: 643 us; the launch traced here: 635 us
  waiting for transfers between devices  323 us (50%)
  matrix products  131 us (20%)
  blocking collectives  104 us (16%)
  other arithmetic  33.2 us (5%)
  starting transfers between devices  26.3 us (4%)
  between operations  14.1 us (2%)
    ppermute x15, waiting for transfers between devices, render_the_limits(): lax.ppermute(w2, axis_name=net_axis, perm=[(pp, (pp - base_arr) % current...  173 us
    reduce_scatter x3, waiting for transfers between devices, project(): full = lax.psum_scatter(part, 'tensor', scatter_dimension=1, tiled=True)  149 us
    psum x1, blocking collectives, body(): score = lax.psum(local_score, 'tensor')  73.9 us
    dot_general x3, matrix products, back_project(): lax.dot_general(left, right, (((1,), (1,)), ((), ())), preferred_element_...  56.5 us
    dot_general x3, matrix products, contract_rows(): lax.dot_general(left, right, (((0,), (0,)), ((), ())), preferred_element_...  38.7 us
    dot_general x3, matrix products, project(): jnp.dot(left, right, preferred_element_type=jnp.float32)  32.3 us
    all_to_all x1, blocking collectives, body(): lax.all_to_all(send, 'expert', split_axis=0, concat_axis=0, tiled=True)  30.5 us
    ppermute x15, starting transfers between devices, render_the_limits(): lax.ppermute(w2, axis_name=net_axis, perm=[(pp, (pp - base_arr) % current...  16.8 us
  transfers between devices with their start and end apart: 20, of which 10 were waited for; matrix products, arithmetic and copies ran while one was open for 24% of the time, Pallas kernels for 0%

profile of v1, /device:TPU:0, one launch (start us, length us, event | category | flops | bytes accessed | tf_op | source)
XLA Modules:
  0.0 635.1 jit_solution(3140959229453547641)
XLA Ops:
  10.7 30.5 %all_to_all.15 = bf16[4,2,80,768]{3,2,1,0:T(8,128)(2,1)S(1)} all-to-all(bf16[4,2,80,768]{3,2,1,0:T(8,128)(2,1)S(1)} %copy.21), channel_id=1, replica_groups=mesh['expert'=4,'tensor'=8] {'expert'}, dimensions={0} | all-to-all | bytes 1966080 | tf_op jit(solution)/shard_map/all_to_all | solution.py:51
  41.3 10.5 %fusion.18 = bf16[320,8192]{1,0:T(8,128)(2,1)} fusion(bf16[320,768]{1,0:T(8,128)(2,1)S(1)} %bitcast.72, bf16[1,768,8192]{2,1,0:T(8,128)(2,1)} %param.20), kind=kOutput, calls=%fused_computation.17 | convolution fusion | flops 4029153280 | bytes 18317312 | tf_op jit(solution)/shard_map/dot_general | solution.py:57
  51.9 10.6 %fusion.15 = bf16[320,8192]{1,0:T(8,128)(2,1)} fusion(bf16[320,768]{1,0:T(8,128)(2,1)S(1)} %bitcast.66, bf16[1,768,8192]{2,1,0:T(8,128)(2,1)} %param.19), kind=kOutput, calls=%fused_computation.16 | convolution fusion | flops 4029153280 | bytes 18317312 | tf_op jit(solution)/shard_map/dot_general | solution.py:57
  62.5 11.2 %fusion.12 = bf16[320,8192]{1,0:T(8,128)(2,1)} fusion(bf16[320,768]{1,0:T(8,128)(2,1)S(1)} %bitcast.67, bf16[1,768,8192]{2,1,0:T(8,128)(2,1)} %param.18), kind=kOutput, calls=%fused_computation.15 | convolution fusion | flops 4029153280 | bytes 18317312 | tf_op jit(solution)/shard_map/dot_general | solution.py:57
  75.2 17.0 %collective-permute-done.9 = bf16[320,768]{1,0:T(8,128)(2,1)S(1)} collective-permute-done((bf16[320,768]{1,0:T(8,128)(2,1)S(1)}, bf16[320,768]{1,0:T(8,128)(2,1)S(1)}, u32[]{:S(2)}, u32[]{:S(2)}) %collective-permute-start.9) | collective-permute-done | bytes 491552 | tf_op jit(solution)/shard_map/ppermute | solution.py:70
  95.3 25.3 %collective-permute-done.12 = bf16[320,768]{1,0:T(8,128)(2,1)S(1)} collective-permute-done((bf16[320,768]{1,0:T(8,128)(2,1)S(1)}, bf16[320,768]{1,0:T(8,128)(2,1)S(1)}, u32[]{:S(2)}, u32[]{:S(2)}) %collective-permute-start.12) | collective-permute-done | bytes 491552 | tf_op jit(solution)/shard_map/ppermute | solution.py:70
  125.4 26.8 %collective-permute-done.13 = bf16[320,1536]{1,0:T(8,128)(2,1)S(1)} collective-permute-done((bf16[320,1536]{1,0:T(8,128)(2,1)S(1)}, bf16[320,1536]{1,0:T(8,128)(2,1)S(1)}, u32[]{:S(2)}, u32[]{:S(2)}) %collective-permute-start.13) | collective-permute-done | bytes 983072 | tf_op jit(solution)/shard_map/ppermute | solution.py:70
  153.9 88.3 %reduce-scatter.6.cloned.1.call-done = bf16[320,1024]{1,0:T(8,128)(2,1)} async-done(((bf16[320,8192]{1,0:T(8,128)(2,1)}), bf16[320,1024]{1,0:T(8,128)(2,1)}) %reduce-scatter.6.cloned.1.call-update) | async-done | bytes 655376 | tf_op jit(solution)/shard_map/reduce_scatter | solution.py:58
  242.3 61.0 %reduce-scatter.4.cloned.1.call-done = bf16[320,1024]{1,0:T(8,128)(2,1)} async-done(((bf16[320,8192]{1,0:T(8,128)(2,1)}), bf16[320,1024]{1,0:T(8,128)(2,1)}) %reduce-scatter.4.cloned.1.call-update) | async-done | bytes 655376 | tf_op jit(solution)/shard_map/reduce_scatter | solution.py:58
  306.7 12.9 %fusion.60 = bf16[320,6144]{1,0:T(8,128)(2,1)} fusion(s32[]{:T(128)S(6)} %select_n.40, bf16[320,768]{1,0:T(8,128)(2,1)S(1)} %bitcast.71, bf16[320,768]{1,0:T(8,128)(2,1)S(1)} %collective-permute-done.9, bf16[320,1536]{1,0:T(8,128)(2,1)} %copy-done.3, bf16[320,3072]{1,0:T(8,128)(2,1)} %collective-permute-done.11), kind=kLoop, calls=%fused_computation.89 | loop fusion | flops 31457280 | bytes 7864324 | tf_op jit(solution)/shard_map/jit(_roll_dynamic)/concatenate | solution.py:77
  324.7 19.3 %convert_bitcast_fusion = bf16[1,6144,1024]{2,1,0:T(8,128)(2,1)} fusion(bf16[320,1024]{1,0:T(8,128)(2,1)S(1)} %get-tuple-element.13, s32[]{:T(128)S(6)} %select_n.40, bf16[320,768]{1,0:T(8,128)(2,1)S(1)} %bitcast.76, bf16[320,768]{1,0:T(8,128)(2,1)} %copy-done.6, bf16[320,1536]{1,0:T(8,128)(2,1)} %copy-done.9, bf16[320,3072]{1,0:T(8,128)(2,1)} %collective-permute-done.14), kind=kOutput, calls=%fused_computation.12 | convolution fusion | flops 4064280576 | bytes 17170436 | tf_op jit(solution)/shard_map/dot_general | solution.py:18
  344.0 20.9 %collective-permute-done.1 = bf16[320,2048]{1,0:T(8,128)(2,1)} collective-permute-done((bf16[320,2048]{1,0:T(8,128)(2,1)}, bf16[320,2048]{1,0:T(8,128)(2,1)}, u32[]{:S(2)}, u32[]{:S(2)}) %collective-permute-start.1) | collective-permute-done | bytes 1310752 | tf_op jit(solution)/shard_map/ppermute | solution.py:70
  368.1 9.7 %convert_bitcast_fusion.2 = bf16[1,6144,1024]{2,1,0:T(8,128)(2,1)} fusion(bf16[320,6144]{1,0:T(8,128)(2,1)S(1)} %copy-done.2, bf16[320,1024]{1,0:T(8,128)(2,1)S(1)} %get-tuple-element.12), kind=kOutput, calls=%fused_computation.14 | convolution fusion | flops 4032823296 | bytes 17170432 | tf_op jit(solution)/shard_map/dot_general | solution.py:18
  383.1 9.7 %convert_bitcast_fusion.1 = bf16[1,6144,1024]{2,1,0:T(8,128)(2,1)} fusion(bf16[320,6144]{1,0:T(8,128)(2,1)S(1)} %copy-done.2, bf16[320,1024]{1,0:T(8,128)(2,1)S(1)} %get-tuple-element.14), kind=kOutput, calls=%fused_computation.13 | convolution fusion | flops 4032823296 | bytes 17170432 | tf_op jit(solution)/shard_map/dot_general | solution.py:18
  392.8 17.9 %collective-permute-done.7 = bf16[320,2048]{1,0:T(8,128)(2,1)S(1)} collective-permute-done((bf16[320,2048]{1,0:T(8,128)(2,1)S(1)}, bf16[320,2048]{1,0:T(8,128)(2,1)S(1)}, u32[]{:S(2)}, u32[]{:S(2)}) %collective-permute-start.7) | collective-permute-done | bytes 1310752 | tf_op jit(solution)/shard_map/ppermute | solution.py:70
  414.9 11.8 %collective-permute-done.4 = bf16[320,2048]{1,0:T(8,128)(2,1)S(1)} collective-permute-done((bf16[320,2048]{1,0:T(8,128)(2,1)S(1)}, bf16[320,2048]{1,0:T(8,128)(2,1)S(1)}, u32[]{:S(2)}, u32[]{:S(2)}) %collective-permute-start.4) | collective-permute-done | bytes 1310752 | tf_op jit(solution)/shard_map/ppermute | solution.py:70
  431.2 18.8 %fusion.77 = bf16[320,768]{1,0:T(8,128)(2,1)} fusion(bf16[1,768,8192]{2,1,0:T(8,128)(2,1)} %param.20, s32[]{:T(128)S(6)} %select_n.34, bf16[320,1024]{1,0:T(8,128)(2,1)S(1)} %get-tuple-element.13, bf16[320,1024]{1,0:T(8,128)(2,1)S(1)} %copy-done.5, bf16[320,2048]{1,0:T(8,128)(2,1)} %collective-permute-done.1, bf16[320,4096]{1,0:T(8,128)(2,1)} %collective-permute-done.2), kind=kOutput, calls=%fused_computation.117 | convolution fusion | flops 4068720640 | bytes 18317316 | tf_op jit(solution)/shard_map/dot_general | solution.py:82
  449.9 4.8 all-to-all-start.1
  454.7 28.0 %collective-permute-done.8 = bf16[320,4096]{1,0:T(8,128)(2,1)} collective-permute-done((bf16[320,4096]{1,0:T(8,128)(2,1)}, bf16[320,4096]{1,0:T(8,128)(2,1)}, u32[]{:S(2)}, u32[]{:S(2)}) %collective-permute-start.8) | collective-permute-done | bytes 2621472 | tf_op jit(solution)/shard_map/ppermute | solution.py:70
  482.7 18.8 %fusion.4 = f32[320,768]{1,0:T(8,128)} fusion(bf16[1,768,8192]{2,1,0:T(8,128)(2,1)} %param.19, s32[]{:T(128)S(6)} %select_n.34, bf16[320,1024]{1,0:T(8,128)(2,1)S(1)} %get-tuple-element.14, bf16[320,1024]{1,0:T(8,128)(2,1)} %collective-permute-done.6, bf16[320,2048]{1,0:T(8,128)(2,1)} %copy-done.8, bf16[320,4096]{1,0:T(8,128)(2,1)} %collective-permute-done.8), kind=kOutput, calls=%fused_computation.4 | convolution fusion | flops 4068474880 | bytes 18808836 | tf_op jit(solution)/shard_map/dot_general | solution.py:82
  501.5 25.6 %collective-permute-done.5 = bf16[320,4096]{1,0:T(8,128)(2,1)} collective-permute-done((bf16[320,4096]{1,0:T(8,128)(2,1)}, bf16[320,4096]{1,0:T(8,128)(2,1)}, u32[]{:S(2)}, u32[]{:S(2)}) %collective-permute-start.5) | collective-permute-done | bytes 2621472 | tf_op jit(solution)/shard_map/ppermute | solution.py:70
  527.1 18.9 %fusion.72 = bf16[320,768]{1,0:T(8,128)(2,1)} fusion(f32[320,768]{1,0:T(8,128)} %fusion.4, bf16[1,768,8192]{2,1,0:T(8,128)(2,1)} %param.18, s32[]{:T(128)S(6)} %select_n.34, bf16[320,1024]{1,0:T(8,128)(2,1)S(1)} %get-tuple-element.12, bf16[320,1024]{1,0:T(8,128)(2,1)} %collective-permute-done.3, bf16[320,2048]{1,0:T(8,128)(2,1)} %copy-done.7, ...), kind=kOutput, calls=%fused_computation.116 | convolution fusion | flops 4068966400 | bytes 19300356 | tf_op jit(solution)/shard_map/dot_general | solution.py:82
  546.0 4.6 all-to-all-start.2
  552.8 73.9 %psum.7 = f32[128,4]{0,1:T(4,128)S(1)} all-reduce(f32[128,4]{0,1:T(4,128)S(1)} %bitcast.81), channel_id=1, replica_groups=mesh['expert'=4,'tensor'=8] {'tensor'}, use_global_device_ids=true, to_apply=%region_6.8 | all-reduce | flops 512 | bytes 4096 | tf_op jit(solution)/shard_map/psum | solution.py:121
  (91 shorter events, 44.3 us)
Async XLA Ops:
  7.2 146.8 %reduce-scatter.8.cloned.1.call-start = ((), (), s32[]{:S(2)}) async-start(), calls=%async_computation.8 | async-start | bytes 5898240 | tf_op jit(solution)/shard_map/reduce_scatter | solution.py:58
  51.8 190.4 %reduce-scatter.6.cloned.1.call-start = ((), (), s32[]{:S(2)}) async-start(), calls=%async_computation.7 | async-start | bytes 5898240 | tf_op jit(solution)/shard_map/reduce_scatter | solution.py:58
  62.5 240.8 %reduce-scatter.4.cloned.1.call-start = ((), (), s32[]{:S(2)}) async-start(), calls=%async_computation.6 | async-start | bytes 5898240 | tf_op jit(solution)/shard_map/reduce_scatter | solution.py:58
  73.7 18.5 %collective-permute-start.9 = (bf16[320,768]{1,0:T(8,128)(2,1)S(1)}, bf16[320,768]{1,0:T(8,128)(2,1)S(1)}, u32[]{:S(2)}, u32[]{:S(2)}) collective-permute-start(bf16[320,768]{1,0:T(8,128)(2,1)S(1)} %bitcast.68), channel_id=1, source_target_pairs={{0,7},{1,0},{2,1},{3,2},{4,3},{5,4},{6,5},{7,6},{8,15},{9,8},{10,9... | collective-permute-start | bytes 1474568 | tf_op jit(solution)/shard_map/ppermute | solution.py:70
  92.3 210.9 %copy-start.11 = (f32[1,1024]{1,0:T(1,128)S(1)}, f32[1,1024]{1,0:T(1,128)}, u32[]{:S(2)}) copy-start(f32[1,1024]{1,0:T(1,128)} %param.23) | copy-start | bytes 12292
  92.3 210.9 %copy-start.12 = (f32[1,1024]{1,0:T(1,128)S(1)}, f32[1,1024]{1,0:T(1,128)}, u32[]{:S(2)}) copy-start(f32[1,1024]{1,0:T(1,128)} %param.22) | copy-start | bytes 12292
  92.3 210.9 %copy-start.13 = (f32[1,1024]{1,0:T(1,128)S(1)}, f32[1,1024]{1,0:T(1,128)}, u32[]{:S(2)}) copy-start(f32[1,1024]{1,0:T(1,128)} %param.21) | copy-start | bytes 12292
  92.3 30.0 %collective-permute-start.10 = (bf16[320,1536]{1,0:T(8,128)(2,1)S(1)}, bf16[320,1536]{1,0:T(8,128)(2,1)S(1)}, u32[]{:S(2)}, u32[]{:S(2)}) collective-permute-start(bf16[320,1536]{1,0:T(8,128)(2,1)S(1)} %pad_maximum_fusion.9), channel_id=1, source_target_pairs={{0,6},{1,7},{2,0},{3,1},{4,2},{5,3},{6,4},{7,5},{8,14},{9,15},{10,... | collective-permute-start | bytes 2949128 | tf_op jit(solution)/shard_map/ppermute | solution.py:70
  93.2 27.4 %collective-permute-start.12 = (bf16[320,768]{1,0:T(8,128)(2,1)S(1)}, bf16[320,768]{1,0:T(8,128)(2,1)S(1)}, u32[]{:S(2)}, u32[]{:S(2)}) collective-permute-start(bf16[320,768]{1,0:T(8,128)(2,1)S(1)} %bitcast.73), channel_id=1, source_target_pairs={{0,7},{1,0},{2,1},{3,2},{4,3},{5,4},{6,5},{7,6},{8,15},{9,8},{10,9... | collective-permute-start | bytes 1474568 | tf_op jit(solution)/shard_map/ppermute | solution.py:70
  120.7 31.6 %collective-permute-start.13 = (bf16[320,1536]{1,0:T(8,128)(2,1)S(1)}, bf16[320,1536]{1,0:T(8,128)(2,1)S(1)}, u32[]{:S(2)}, u32[]{:S(2)}) collective-permute-start(bf16[320,1536]{1,0:T(8,128)(2,1)S(1)} %pad_maximum_fusion.10), channel_id=1, source_target_pairs={{0,6},{1,7},{2,0},{3,1},{4,2},{5,3},{6,4},{7,5},{8,14},{9,15},{10,... | collective-permute-start | bytes 2949128 | tf_op jit(solution)/shard_map/ppermute | solution.py:70
  124.8 181.9 %collective-permute-start.11 = (bf16[320,3072]{1,0:T(8,128)(2,1)}, bf16[320,3072]{1,0:T(8,128)(2,1)}, u32[]{:S(2)}, u32[]{:S(2)}) collective-permute-start(bf16[320,3072]{1,0:T(8,128)(2,1)} %pad_maximum_fusion.3), channel_id=1, source_target_pairs={{0,4},{1,5},{2,6},{3,7},{4,0},{5,1},{6,2},{7,3},{8,12},{9,13},{10,... | collective-permute-start | bytes 5898248 | tf_op jit(solution)/shard_map/ppermute | solution.py:70
  153.9 170.8 %collective-permute-start.14 = (bf16[320,3072]{1,0:T(8,128)(2,1)}, bf16[320,3072]{1,0:T(8,128)(2,1)}, u32[]{:S(2)}, u32[]{:S(2)}) collective-permute-start(bf16[320,3072]{1,0:T(8,128)(2,1)} %pad_maximum_fusion.4), channel_id=1, source_target_pairs={{0,4},{1,5},{2,6},{3,7},{4,0},{5,1},{6,2},{7,3},{8,12},{9,13},{10,... | collective-permute-start | bytes 5898248 | tf_op jit(solution)/shard_map/ppermute | solution.py:70
  305.8 15.5 %collective-permute-start = (bf16[320,1024]{1,0:T(8,128)(2,1)S(1)}, bf16[320,1024]{1,0:T(8,128)(2,1)S(1)}, u32[]{:S(2)}, u32[]{:S(2)}) collective-permute-start(bf16[320,1024]{1,0:T(8,128)(2,1)S(1)} %get-tuple-element.13), channel_id=1, source_target_pairs={{0,7},{1,0},{2,1},{3,2},{4,3},{5,4},{6,5},{7,6},{8,15},{9,8},{10,9... | collective-permute-start | bytes 1966088 | tf_op jit(solution)/shard_map/ppermute | solution.py:70
  319.7 61.8 %collective-permute-start.3 = (bf16[320,1024]{1,0:T(8,128)(2,1)S(1)}, bf16[320,1024]{1,0:T(8,128)(2,1)}, u32[]{:S(2)}, u32[]{:S(2)}) collective-permute-start(bf16[320,1024]{1,0:T(8,128)(2,1)S(1)} %get-tuple-element.12), channel_id=1, source_target_pairs={{0,7},{1,0},{2,1},{3,2},{4,3},{5,4},{6,5},{7,6},{8,15},{9,8},{10,9... | collective-permute-start | bytes 1966088 | tf_op jit(solution)/shard_map/ppermute | solution.py:70
  320.5 57.3 %collective-permute-start.6 = (bf16[320,1024]{1,0:T(8,128)(2,1)S(1)}, bf16[320,1024]{1,0:T(8,128)(2,1)}, u32[]{:S(2)}, u32[]{:S(2)}) collective-permute-start(bf16[320,1024]{1,0:T(8,128)(2,1)S(1)} %get-tuple-element.14), channel_id=1, source_target_pairs={{0,7},{1,0},{2,1},{3,2},{4,3},{5,4},{6,5},{7,6},{8,15},{9,8},{10,9... | collective-permute-start | bytes 1966088 | tf_op jit(solution)/shard_map/ppermute | solution.py:70
  323.3 41.6 %collective-permute-start.1 = (bf16[320,2048]{1,0:T(8,128)(2,1)}, bf16[320,2048]{1,0:T(8,128)(2,1)}, u32[]{:S(2)}, u32[]{:S(2)}) collective-permute-start(bf16[320,2048]{1,0:T(8,128)(2,1)} %pad_maximum_fusion.5), channel_id=1, source_target_pairs={{0,6},{1,7},{2,0},{3,1},{4,2},{5,3},{6,4},{7,5},{8,14},{9,15},{10,... | collective-permute-start | bytes 3932168 | tf_op jit(solution)/shard_map/ppermute | solution.py:70
  366.6 64.6 %collective-permute-start.2 = (bf16[320,4096]{1,0:T(8,128)(2,1)S(1)}, bf16[320,4096]{1,0:T(8,128)(2,1)}, u32[]{:S(2)}, u32[]{:S(2)}) collective-permute-start(bf16[320,4096]{1,0:T(8,128)(2,1)S(1)} %pad_maximum_fusion), channel_id=1, source_target_pairs={{0,4},{1,5},{2,6},{3,7},{4,0},{5,1},{6,2},{7,3},{8,12},{9,13},{10,... | collective-permute-start | bytes 7864328 | tf_op jit(solution)/shard_map/ppermute | solution.py:70
  379.0 31.7 %collective-permute-start.7 = (bf16[320,2048]{1,0:T(8,128)(2,1)S(1)}, bf16[320,2048]{1,0:T(8,128)(2,1)S(1)}, u32[]{:S(2)}, u32[]{:S(2)}) collective-permute-start(bf16[320,2048]{1,0:T(8,128)(2,1)S(1)} %pad_maximum_fusion.7), channel_id=1, source_target_pairs={{0,6},{1,7},{2,0},{3,1},{4,2},{5,3},{6,4},{7,5},{8,14},{9,15},{10,... | collective-permute-start | bytes 3932168 | tf_op jit(solution)/shard_map/ppermute | solution.py:70
  382.6 44.1 %collective-permute-start.4 = (bf16[320,2048]{1,0:T(8,128)(2,1)S(1)}, bf16[320,2048]{1,0:T(8,128)(2,1)S(1)}, u32[]{:S(2)}, u32[]{:S(2)}) collective-permute-start(bf16[320,2048]{1,0:T(8,128)(2,1)S(1)} %pad_maximum_fusion.6), channel_id=1, source_target_pairs={{0,6},{1,7},{2,0},{3,1},{4,2},{5,3},{6,4},{7,5},{8,14},{9,15},{10,... | collective-permute-start | bytes 3932168 | tf_op jit(solution)/shard_map/ppermute | solution.py:70
  414.0 68.6 %collective-permute-start.8 = (bf16[320,4096]{1,0:T(8,128)(2,1)}, bf16[320,4096]{1,0:T(8,128)(2,1)}, u32[]{:S(2)}, u32[]{:S(2)}) collective-permute-start(bf16[320,4096]{1,0:T(8,128)(2,1)} %pad_maximum_fusion.2), channel_id=1, source_target_pairs={{0,4},{1,5},{2,6},{3,7},{4,0},{5,1},{6,2},{7,3},{8,12},{9,13},{10,... | collective-permute-start | bytes 7864328 | tf_op jit(solution)/shard_map/ppermute | solution.py:70
  430.6 96.5 %collective-permute-start.5 = (bf16[320,4096]{1,0:T(8,128)(2,1)}, bf16[320,4096]{1,0:T(8,128)(2,1)}, u32[]{:S(2)}, u32[]{:S(2)}) collective-permute-start(bf16[320,4096]{1,0:T(8,128)(2,1)} %pad_maximum_fusion.1), channel_id=1, source_target_pairs={{0,4},{1,5},{2,6},{3,7},{4,0},{5,1},{6,2},{7,3},{8,12},{9,13},{10,... | collective-permute-start | bytes 7864328 | tf_op jit(solution)/shard_map/ppermute | solution.py:70
  449.9 96.1 %all-to-all-start.1 = ((bf16[4,80,768]{2,1,0:T(8,128)(2,1)}), bf16[4,80,768]{2,1,0:T(8,128)(2,1)S(1)}, u32[]{:S(2)}, u32[]{:S(2)}) async-start(bf16[4,80,768]{2,1,0:T(8,128)(2,1)} %bitcast.77), calls=%async_computation.3 | async-start | bytes 983040 | tf_op jit(solution)/shard_map/all_to_all | solution.py:87
  527.1 101.3 %copy-start.1 = (bf16[128,768]{1,0:T(8,128)(2,1)S(1)}, bf16[128,768]{1,0:T(8,128)(2,1)}, u32[]{:S(2)}) copy-start(bf16[128,768]{1,0:T(8,128)(2,1)} %param.14) | copy-start | bytes 589828
  546.0 81.4 %all-to-all-start.2 = ((bf16[4,80,768]{2,1,0:T(8,128)(2,1)}), bf16[4,80,768]{2,1,0:T(8,128)(2,1)S(1)}, u32[]{:S(2)}, u32[]{:S(2)}) async-start(bf16[4,80,768]{2,1,0:T(8,128)(2,1)} %bitcast.14), calls=%async_computation.5 | async-start | bytes 983040 | tf_op jit(solution)/shard_map/all_to_all | solution.py:87
  (11 other events, 252.2 us)
Sparse Core Ops, SparseCore 0:
  52.0 94.1 reduce-scatter.7
  150.1 92.0 reduce-scatter.5
  246.2 56.9 reduce-scatter.3
